TPU v7x, 32 devices: a whole 2x2x4 slice. The times are simulated.
32 devices in a mesh: area: 8 (over z, x), scen: 4 (over y, core).
Axes of the slice: x: 2, y: 2, z: 4, core: 2. Of those that a mesh axis runs over, the one named last changes fastest.
Arguments:
- injection: float32 [8, 128, 4096], P('area', 'scen'), may hold values from -6 to 6
- kkt_factor: bfloat16 [8, 4096, 4096], P('area', 'scen'), may hold values from -0.09375 to 0.09375
- dual_price: float32 [8, 128, 512], P('area', 'scen'), may hold values from -6 to 6
- area_size: int32 [8], replicated, may hold values from 1024 to 4096, as said below
- bnd_bus: int32 [8, 512], replicated, may hold values from 0 to 4095, as said below
- peer_end: int32 [8, 512], replicated, may hold values from 0 to 4095, as said below
Outputs:
- angles: float32 [8, 128, 4096], P('area', 'scen')
- dual_out: float32 [8, 128, 512], P('area', 'scen')
- consensus: float32 [8, 128, 512], P('area', 'scen')
Inputs may be any that keep to these rules, and one draw needn't show every extreme that they name: `area_size`: one area has exactly 4096 live buses and another exactly 1024. `bnd_bus`: the buses of one area's ends are distinct and lie below that area's size; they include bus 0 and the area's last live bus. peer_end is a pairing: the peer of an end's peer is the end itself, and the two ends lie in different areas. The ends of area a form 4 tie sets of 128 consecutive ends; tie set g of area a is paired whole with tie set g of area a XOR s_g, where s_g is nonzero, the same for all areas, and the 4 values s_g differ.
All inputs are finite; a program needn't handle non-finite values.
Results may differ from a plain program's by a relative error of at most 0.0043.
Values may be sent and summed in bfloat16 or wider, within the bound.
No kernel may reach another device: no remote copies, remote signals or barrier semaphores. Data moves between devices by JAX's collectives and lax.ppermute only.
A program may use at most 128 MiB of HBM per device.

v0:
```python
import jax
import jax.numpy as jnp
from jax import lax
from jax.sharding import PartitionSpec as P

CAP = 128
ITERS = 2
PENALTY = 1.5
PROXIMAL = 0.5


def shards(injection, kkt_factor, dual_price, area_size, bnd_bus, peer_end):
    area_id = lax.axis_index("area")
    band_index = lax.axis_index("scen")
    areas_all = lax.axis_size("area")
    factor = kkt_factor[0]
    band_rows = factor.shape[0]
    width = factor.shape[1]
    columns = injection.shape[1]
    ends_total = bnd_bus.shape[1]
    slot_count = CAP
    groups = ends_total // slot_count
    size_here = area_size[area_id]
    live_mask = (jnp.arange(width) < size_here).astype(jnp.float32)
    band_mask = (band_index * band_rows + jnp.arange(band_rows) < size_here).astype(jnp.float32)[
        None, :
    ]
    buses = bnd_bus[area_id]
    peers = peer_end[area_id]
    group_mate = peers.reshape(groups, slot_count)[:, 0] // ends_total
    group_ids = jnp.arange(groups)
    owner_dev = 8 * (jnp.minimum(area_id, group_mate) // 8) + group_ids
    injection_here = injection[0]
    dual_here = dual_price[0]
    consensus = jnp.zeros((columns, ends_total), jnp.float32)
    held = jnp.zeros((columns, areas_all, slot_count), jnp.float32)
    angles = jnp.zeros((columns, width), jnp.float32)
    for sweep in range(ITERS):
        pushed = dual_here - PENALTY * consensus
        spread = jnp.zeros((columns, width), jnp.float32).at[:, buses].add(pushed)
        right_side = ((injection_here - spread) * live_mask).astype(jnp.bfloat16)
        projected = jnp.dot(
            lax.all_gather(right_side, "scen", axis=0, tiled=True),
            factor.T,
            preferred_element_type=jnp.float32,
        )
        projected = (projected * band_mask).astype(jnp.bfloat16)
        angles = (
            lax.psum_scatter(
                jnp.dot(projected, factor, preferred_element_type=jnp.float32),
                "scen",
                scatter_dimension=0,
                tiled=True,
            )
            * live_mask
        )
        end_angles = angles[:, buses]
        stacked = jnp.stack([end_angles, dual_here]).reshape(2, columns, groups, slot_count)
        source_group = jnp.minimum(area_id % 8, groups - 1)
        source_peers = lax.dynamic_slice_in_dim(peer_end, source_group * slot_count, slot_count, 1)
        source_flat = (source_peers // ends_total * slot_count + source_peers % slot_count).reshape(
            -1
        )
        outgoing = (
            jnp.zeros((2, columns, areas_all, slot_count), jnp.float32)
            .at[:, :, owner_dev]
            .set(stacked)
        )
        incoming = lax.all_to_all(outgoing, "area", split_axis=2, concat_axis=2, tiled=True)
        flat_in = incoming.reshape(2, columns, areas_all * slot_count)
        mate_vals = flat_in[:, :, source_flat].reshape(2, columns, areas_all, slot_count)
        held = (
            PENALTY * (incoming[0] + mate_vals[0]) + (incoming[1] + mate_vals[1]) + PROXIMAL * held
        ) / (2.0 * PENALTY + PROXIMAL)
        returned = lax.all_to_all(held, "area", split_axis=1, concat_axis=1, tiled=True)
        consensus = returned[:, owner_dev, :].reshape(columns, ends_total)
        dual_here = dual_here + PENALTY * (end_angles - consensus)
    return (angles[None], dual_here[None], consensus[None])


def solution(mesh):
    return jax.shard_map(
        shards,
        mesh=mesh,
        in_specs=(
            P("area", "scen", None),
            P("area", "scen", None),
            P("area", "scen", None),
            P(),
            P(),
            P(),
        ),
        out_specs=(P("area", "scen", None), P("area", "scen", None), P("area", "scen", None)),
        check_vma=False,
    )
```

profile of v0, /device:TPU:0, one launch (start us, length us, event | category | flops | bytes accessed | tf_op | source)
XLA Modules:
  0.0 220.0 jit_solution(10403555091593370773)
XLA Ops:
  7.2 1.2 dynamic_slice.14
  10.8 2.8 %scatter_custom_fusion = f32[32,4096]{0,1:T(8,128)S(1)} fusion(s32[512]{0:T(512)S(1)} %bitcast.168, f32[]{:T(128)} %constant.82.clone.1, f32[1,32,512]{1,2,0:T(8,128)S(1)} %copy.107), kind=kCustom, calls=%fused_computation.24 | custom fusion | flops 16384 | bytes 786436 | tf_op jit(solution)/shard_map/scatter-add | solution.py:40
  15.7 18.9 %all-gather.3.cloned.1.call-done = bf16[128,4096]{1,0:T(8,128)(2,1)} async-done(((bf16[32,4096]{1,0:T(8,128)(2,1)}), bf16[128,4096]{1,0:T(8,128)(2,1)}) %all-gather.3.cloned.1.call-update) | async-done | bytes 1048592 | tf_op jit(solution)/shard_map/all_gather | solution.py:43
  34.6 11.4 %fusion.4 = f32[128,4096]{1,0:T(8,128)} fusion(bf16[1,1024,4096]{2,1,0:T(8,128)(2,1)} %param.7, bf16[128,4096]{1,0:T(8,128)(2,1)} %all-gather.3.cloned.1.call-done, f32[1024]{0:T(1024)S(1)} %fusion.57), kind=kOutput, calls=%fused_computation.14 | convolution fusion | flops 2147745792 | bytes 11538432 | tf_op jit(solution)/shard_map/dot_general | solution.py:50
  46.9 30.4 %reduce-scatter.3.cloned.1.call-done = f32[32,4096]{1,0:T(8,128)} async-done(((f32[128,4096]{1,0:T(8,128)}), f32[32,4096]{1,0:T(8,128)}) %reduce-scatter.3.cloned.1.call-update) | async-done | bytes 524304 | tf_op jit(solution)/shard_map/reduce_scatter | solution.py:49
  77.3 1.1 broadcast_multiply_fusion.1
  79.0 1.0 gather_fusion
  81.6 5.5 %all-to-all-start = ((f32[2,32,8,128]{3,1,0,2:T(8,128)}), f32[2,32,8,128]{3,1,0,2:T(8,128)S(1)}, u32[]{:S(2)}, u32[]{:S(2)}) async-start(f32[2,32,8,128]{3,1,0,2:T(8,128)} %copy.112), calls=%async_computation.1 | async-start | bytes 524288 | tf_op jit(solution)/shard_map/all_to_all | solution.py:69
  87.9 8.0 %all-to-all-done = f32[2,32,8,128]{3,1,0,2:T(8,128)S(1)} async-done(((f32[2,32,8,128]{3,1,0,2:T(8,128)}), f32[2,32,8,128]{3,1,0,2:T(8,128)S(1)}, u32[]{:S(2)}, u32[]{:S(2)}) %all-to-all-start) | async-done | bytes 262176 | tf_op jit(solution)/shard_map/all_to_all | solution.py:69
  96.5 3.6 %gather_fusion.1 = f32[1024,2,32]{2,1,0:T(2,128)S(1)} fusion(f32[2,32,1024]{1,0,2:T(2,128)S(1)} %bitcast.162, s32[1024]{0:T(1024)S(1)} %broadcast_clamp_fusion), kind=kCustom, calls=%fused_computation.1 | custom fusion | bytes 528384 | tf_op jit(solution)/shard_map/gather | solution.py:71
  101.9 3.6 %all-to-all-start.1 = ((f32[32,8,128]{2,0,1:T(8,128)}), f32[32,8,128]{2,0,1:T(8,128)S(1)}, u32[]{:S(2)}, u32[]{:S(2)}) async-start(f32[32,8,128]{2,0,1:T(8,128)} %get-tuple-element.18), calls=%async_computation.2 | async-start | bytes 262144 | tf_op jit(solution)/shard_map/all_to_all | solution.py:75
  105.6 7.3 %all-to-all-done.1 = f32[32,8,128]{2,0,1:T(8,128)S(1)} async-done(((f32[32,8,128]{2,0,1:T(8,128)}), f32[32,8,128]{2,0,1:T(8,128)S(1)}, u32[]{:S(2)}, u32[]{:S(2)}) %all-to-all-start.1) | async-done | bytes 131104 | tf_op jit(solution)/shard_map/all_to_all | solution.py:75
  113.6 2.9 %scatter_custom_fusion.2 = f32[32,4096]{0,1:T(8,128)S(1)} fusion(s32[512]{0:T(512)} %bitcast.170, f32[]{:T(128)} %constant.82.clone.1, f32[32,512]{0,1:T(8,128)S(1)} %fusion.40), kind=kCustom, calls=%fused_computation.22 | custom fusion | flops 16384 | bytes 590336 | tf_op jit(solution)/shard_map/scatter-add | solution.py:40
  116.5 1.4 copy.122
  117.9 2.0 fusion.31
  120.1 13.5 %all-gather.5.cloned.1.call-done = bf16[128,4096]{1,0:T(8,128)(2,1)} async-done(((bf16[32,4096]{1,0:T(8,128)(2,1)}), bf16[128,4096]{1,0:T(8,128)(2,1)}) %all-gather.5.cloned.1.call-update) | async-done | bytes 1048592 | tf_op jit(solution)/shard_map/all_gather | solution.py:43
  133.6 11.4 %fusion = f32[128,4096]{1,0:T(8,128)} fusion(bf16[1,1024,4096]{2,1,0:T(8,128)(2,1)} %param.7, bf16[128,4096]{1,0:T(8,128)(2,1)} %all-gather.5.cloned.1.call-done, f32[1024]{0:T(1024)S(1)} %fusion.57), kind=kOutput, calls=%fused_computation.10 | convolution fusion | flops 2147745792 | bytes 11538432 | tf_op jit(solution)/shard_map/dot_general | solution.py:50
  145.2 31.2 %reduce-scatter.5.cloned.1.call-done = f32[32,4096]{1,0:T(8,128)} async-done(((f32[128,4096]{1,0:T(8,128)}), f32[32,4096]{1,0:T(8,128)}) %reduce-scatter.5.cloned.1.call-update) | async-done | bytes 524304 | tf_op jit(solution)/shard_map/reduce_scatter | solution.py:49
  176.4 1.1 broadcast_multiply_fusion
  178.1 1.0 gather_fusion.3
  180.1 14.0 %all_to_all.20 = f32[2,32,8,128]{3,1,0,2:T(8,128)S(1)} all-to-all(f32[2,32,8,128]{3,1,0,2:T(8,128)S(1)} %copy.128), channel_id=1, replica_groups=mesh['area'=8,'scen'=4] {'area'}, dimensions={2} | all-to-all | bytes 524288 | tf_op jit(solution)/shard_map/all_to_all | solution.py:69
  194.8 3.6 %gather_fusion.4 = f32[1024,2,32]{2,1,0:T(2,128)S(1)} fusion(f32[2,32,1024]{1,0,2:T(2,128)S(1)} %bitcast.161, s32[1024]{0:T(1024)S(1)} %copy-done.4), kind=kCustom, calls=%fused_computation.4 | custom fusion | bytes 528384 | tf_op jit(solution)/shard_map/gather | solution.py:71
  200.2 3.6 %all-to-all-start.3 = ((f32[32,8,128]{2,0,1:T(8,128)}), f32[32,8,128]{2,0,1:T(8,128)S(1)}, u32[]{:S(2)}, u32[]{:S(2)}) async-start(f32[32,8,128]{2,0,1:T(8,128)} %fusion.46), calls=%async_computation.5 | async-start | bytes 262144 | tf_op jit(solution)/shard_map/all_to_all | solution.py:75
  204.6 6.5 %all-to-all-done.3 = f32[32,8,128]{2,0,1:T(8,128)S(1)} async-done(((f32[32,8,128]{2,0,1:T(8,128)}), f32[32,8,128]{2,0,1:T(8,128)S(1)}, u32[]{:S(2)}, u32[]{:S(2)}) %all-to-all-start.3) | async-done | bytes 131104 | tf_op jit(solution)/shard_map/all_to_all | solution.py:75
  (75 shorter events, 19.0 us)
Async XLA Ops:
  7.2 27.4 %all-gather.3.cloned.1.call-start = ((), (), s32[]{:S(2)}) async-start(), calls=%async_computation.6 | async-start | bytes 1310720 | tf_op jit(solution)/shard_map/all_gather | solution.py:43
  9.2 37.6 %copy-start.8 = (s32[512,1]{0,1:T(1,128)}, s32[512,1]{0,1:T(1,128)S(1)}, u32[]{:S(2)}) copy-start(s32[512,1]{0,1:T(1,128)S(1)} %compare_select_fusion.1) | copy-start | bytes 6148
  10.8 3.4 %copy-start.1 = (f32[1,32,4096]{2,1,0:T(8,128)S(1)}, f32[1,32,4096]{2,1,0:T(8,128)}, u32[]{:S(2)}) copy-start(f32[1,32,4096]{2,1,0:T(8,128)} %param.6) | copy-start | bytes 1572868
  15.0 62.4 %reduce-scatter.3.cloned.1.call-start = ((), (), s32[]{:S(2)}) async-start(), calls=%async_computation.7 | async-start | bytes 2621440 | tf_op jit(solution)/shard_map/reduce_scatter | solution.py:49
  46.0 0.9 copy-start.2
  46.8 33.3 %copy-start.5 = (s32[1024]{0:T(1024)}, s32[1024]{0:T(1024)S(1)}, u32[]{:S(2)}) copy-start(s32[1024]{0:T(1024)S(1)} %pad_clamp_fusion.1) | copy-start | bytes 12292
  46.9 58.7 %copy-start.7 = (s32[4]{0:T(128)}, s32[4]{0:T(128)S(1)}, u32[]{:S(2)}) copy-start(s32[4]{0:T(128)S(1)} %fusion.65) | copy-start | bytes 52
  81.6 14.3 %all-to-all-start = ((f32[2,32,8,128]{3,1,0,2:T(8,128)}), f32[2,32,8,128]{3,1,0,2:T(8,128)S(1)}, u32[]{:S(2)}, u32[]{:S(2)}) async-start(f32[2,32,8,128]{3,1,0,2:T(8,128)} %copy.112), calls=%async_computation.1 | async-start | bytes 524288 | tf_op jit(solution)/shard_map/all_to_all | solution.py:69
  87.9 13.2 %copy-start.3 = (s32[1024]{0:T(1024)}, s32[1024]{0:T(1024)S(1)}, u32[]{:S(2)}) copy-start(s32[1024]{0:T(1024)S(1)} %broadcast_clamp_fusion) | copy-start | bytes 12292
  101.9 10.9 %all-to-all-start.1 = ((f32[32,8,128]{2,0,1:T(8,128)}), f32[32,8,128]{2,0,1:T(8,128)S(1)}, u32[]{:S(2)}, u32[]{:S(2)}) async-start(f32[32,8,128]{2,0,1:T(8,128)} %get-tuple-element.18), calls=%async_computation.2 | async-start | bytes 262144 | tf_op jit(solution)/shard_map/all_to_all | solution.py:75
  105.5 28.1 %all-gather.5.cloned.1.call-start = ((), (), s32[]{:S(2)}) async-start(), calls=%async_computation.8 | async-start | bytes 1310720 | tf_op jit(solution)/shard_map/all_gather | solution.py:43
  105.6 12.3 %copy-start.9 = (s32[1024]{0:T(1024)}, s32[1024]{0:T(1024)S(1)}, u32[]{:S(2)}) copy-start(s32[1024]{0:T(1024)S(1)} %pad_clamp_fusion) | copy-start | bytes 12292
  119.9 56.5 %reduce-scatter.5.cloned.1.call-start = ((), (), s32[]{:S(2)}) async-start(), calls=%async_computation.9 | async-start | bytes 2621440 | tf_op jit(solution)/shard_map/reduce_scatter | solution.py:49
  145.1 33.0 %copy-start.6 = (s32[1024]{0:T(1024)S(1)}, s32[1024]{0:T(1024)}, u32[]{:S(2)}) copy-start(s32[1024]{0:T(1024)} %copy-done.5) | copy-start | bytes 12292
  179.1 15.6 %copy-start.4 = (s32[1024]{0:T(1024)S(1)}, s32[1024]{0:T(1024)}, u32[]{:S(2)}) copy-start(s32[1024]{0:T(1024)} %copy-done.3) | copy-start | bytes 12292
  198.3 5.5 %copy-start = (f32[32,4096]{1,0:T(8,128)S(1)}, f32[32,4096]{1,0:T(8,128)}, u32[]{:S(2)}) copy-start(f32[32,4096]{1,0:T(8,128)} %reduce-scatter.5.cloned.1.call-done) | copy-start | bytes 1572868
  200.2 10.9 %all-to-all-start.3 = ((f32[32,8,128]{2,0,1:T(8,128)}), f32[32,8,128]{2,0,1:T(8,128)S(1)}, u32[]{:S(2)}, u32[]{:S(2)}) async-start(f32[32,8,128]{2,0,1:T(8,128)} %fusion.46), calls=%async_computation.5 | async-start | bytes 262144 | tf_op jit(solution)/shard_map/all_to_all | solution.py:75
Sparse Core Ops, SparseCore 0:
  15.1 19.4 all-gather.2
  46.1 31.1 reduce-scatter.2
  120.0 13.5 all-gather.4
  145.2 31.1 reduce-scatter.4
where the time goes:
time: 221 us; the launch traced here: 220 us
  waiting for transfers between devices  116 us (52%)
  local copies, waits for them, and re-layouts  24.3 us (11%)
  matrix products  22.8 us (10%)
  other arithmetic  15.9 us (7%)
  between operations  14.2 us (6%)
  blocking collectives  14 us (6%)
  starting transfers between devices  13 us (6%)
    reduce_scatter x2, waiting for transfers between devices, shards(): lax.psum_scatter(jnp.dot(projected, factor, preferred_element_type=jnp.fl...  61.6 us
    all_gather x2, waiting for transfers between devices, shards(): lax.all_gather(right_side, 'scen', axis=0, tiled=True)  32.3 us
    dot_general x2, matrix products, shards(): jnp.dot(projected, factor, preferred_element_type=jnp.float32)  22.8 us
    all_to_all x1, blocking collectives, shards(): lax.all_to_all(outgoing, 'area', split_axis=2, concat_axis=2, tiled=True)  14 us
    all_to_all x2, waiting for transfers between devices, shards(): lax.all_to_all(held, 'area', split_axis=1, concat_axis=1, tiled=True)  13.8 us
    all_to_all x1, waiting for transfers between devices, shards(): lax.all_to_all(outgoing, 'area', split_axis=2, concat_axis=2, tiled=True)  8.02 us
    all_to_all x2, starting transfers between devices, shards(): lax.all_to_all(held, 'area', split_axis=1, concat_axis=1, tiled=True)  7.17 us
    gather x2, local copies, waits for them, and re-layouts, shards(): flat_in[:, :, source_flat].reshape(2, columns, areas_all, slot_count)  7.11 us
  transfers between devices with their start and end apart: 7, of which 7 were waited for; matrix products, arithmetic and copies ran while one was open for 1% of the time, Pallas kernels for 0%

commit v1 on v0

--- a/solution.py
+++ b/solution.py
@@ -72,7 +72,10 @@
         held = (
             PENALTY * (incoming[0] + mate_vals[0]) + (incoming[1] + mate_vals[1]) + PROXIMAL * held
         ) / (2.0 * PENALTY + PROXIMAL)
-        returned = lax.all_to_all(held, "area", split_axis=1, concat_axis=1, tiled=True)
+        returned = jnp.concatenate(
+            lax.all_to_all(jnp.stack(jnp.split(held, lax.axis_size("area"), axis=1)), "area", 0, 0),
+            axis=1,
+        )
         consensus = returned[:, owner_dev, :].reshape(columns, ends_total)
         dual_here = dual_here + PENALTY * (end_angles - consensus)
     return (angles[None], dual_here[None], consensus[None])

time: 221 us -> 230 us (1.041)
  local copies, waits for them, and re-layouts: 24.3 us -> 34.6 us
    unnamed x23 -> x37, local copies, waits for them, and re-layouts: 2.49 us -> 10.9 us
where the time goes in v1:
time: 230 us; the launch traced here: 229 us
  waiting for transfers between devices  116 us (50%)
  local copies, waits for them, and re-layouts  34.6 us (15%)
  matrix products  22.8 us (10%)
  other arithmetic  15 us (7%)
  between operations  14.3 us (6%)
  blocking collectives  14.1 us (6%)
  starting transfers between devices  12.8 us (6%)
    reduce_scatter x2, waiting for transfers between devices, shards(): lax.psum_scatter(jnp.dot(projected, factor, preferred_element_type=jnp.fl...  61.6 us
    all_gather x2, waiting for transfers between devices, shards(): lax.all_gather(right_side, 'scen', axis=0, tiled=True)  32.5 us
    dot_general x2, matrix products, shards(): jnp.dot(projected, factor, preferred_element_type=jnp.float32)  22.8 us
    all_to_all x1, blocking collectives, shards(): lax.all_to_all(outgoing, 'area', split_axis=2, concat_axis=2, tiled=True)  14.1 us
    all_to_all x2, waiting for transfers between devices, shards(): lax.all_to_all(jnp.stack(jnp.split(held, lax.axis_size('area'), axis=1)),...  13.8 us
    unnamed x37, local copies, waits for them, and re-layouts  10.9 us
    all_to_all x1, waiting for transfers between devices, shards(): lax.all_to_all(outgoing, 'area', split_axis=2, concat_axis=2, tiled=True)  8.02 us
    gather x2, local copies, waits for them, and re-layouts, shards(): flat_in[:, :, source_flat].reshape(2, columns, areas_all, slot_count)  7.6 us
  transfers between devices with their start and end apart: 7, of which 7 were waited for; matrix products, arithmetic and copies ran while one was open for 1% of the time, Pallas kernels for 0%

profile of v1, /device:TPU:0, one launch (start us, length us, event | category | flops | bytes accessed | tf_op | source)
XLA Modules:
  0.0 229.5 jit_solution(4439129182628111527)
XLA Ops:
  7.2 1.2 dynamic_slice.14
  10.8 2.8 %scatter_custom_fusion = f32[32,4096]{0,1:T(8,128)S(1)} fusion(s32[512]{0:T(512)S(1)} %bitcast.228, f32[]{:T(128)} %constant.82.clone.1, f32[1,32,512]{1,2,0:T(8,128)S(1)} %copy.78), kind=kCustom, calls=%fused_computation.24 | custom fusion | flops 16384 | bytes 786436 | tf_op jit(solution)/shard_map/scatter-add | solution.py:40
  15.7 18.9 %all-gather.3.cloned.1.call-done = bf16[128,4096]{1,0:T(8,128)(2,1)} async-done(((bf16[32,4096]{1,0:T(8,128)(2,1)}), bf16[128,4096]{1,0:T(8,128)(2,1)}) %all-gather.3.cloned.1.call-update) | async-done | bytes 1048592 | tf_op jit(solution)/shard_map/all_gather | solution.py:43
  34.6 11.4 %fusion.4 = f32[128,4096]{1,0:T(8,128)} fusion(bf16[1,1024,4096]{2,1,0:T(8,128)(2,1)} %param.7, bf16[128,4096]{1,0:T(8,128)(2,1)} %all-gather.3.cloned.1.call-done, f32[1024]{0:T(1024)S(1)} %fusion.57), kind=kOutput, calls=%fused_computation.14 | convolution fusion | flops 2147745792 | bytes 11538432 | tf_op jit(solution)/shard_map/dot_general | solution.py:50
  46.9 30.4 %reduce-scatter.3.cloned.1.call-done = f32[32,4096]{1,0:T(8,128)} async-done(((f32[128,4096]{1,0:T(8,128)}), f32[32,4096]{1,0:T(8,128)}) %reduce-scatter.3.cloned.1.call-update) | async-done | bytes 524304 | tf_op jit(solution)/shard_map/reduce_scatter | solution.py:49
  77.3 1.1 broadcast_multiply_fusion.1
  79.0 1.0 gather_fusion
  81.6 5.5 %all-to-all-start = ((f32[2,32,8,128]{3,1,0,2:T(8,128)}), f32[2,32,8,128]{3,1,0,2:T(8,128)S(1)}, u32[]{:S(2)}, u32[]{:S(2)}) async-start(f32[2,32,8,128]{3,1,0,2:T(8,128)} %copy.83), calls=%async_computation.1 | async-start | bytes 524288 | tf_op jit(solution)/shard_map/all_to_all | solution.py:69
  87.9 8.0 %all-to-all-done = f32[2,32,8,128]{3,1,0,2:T(8,128)S(1)} async-done(((f32[2,32,8,128]{3,1,0,2:T(8,128)}), f32[2,32,8,128]{3,1,0,2:T(8,128)S(1)}, u32[]{:S(2)}, u32[]{:S(2)}) %all-to-all-start) | async-done | bytes 262176 | tf_op jit(solution)/shard_map/all_to_all | solution.py:69
  96.5 3.6 %gather_fusion.1 = f32[1024,2,32]{2,1,0:T(2,128)S(1)} fusion(f32[2,32,1024]{1,0,2:T(2,128)S(1)} %bitcast.204, s32[1024]{0:T(1024)S(1)} %broadcast_clamp_fusion), kind=kCustom, calls=%fused_computation.1 | custom fusion | bytes 528384 | tf_op jit(solution)/shard_map/gather | solution.py:71
  106.4 3.6 %all-to-all-start.1 = ((f32[8,32,1,128]{3,1,2,0:T(8,128)}), f32[8,32,1,128]{3,1,2,0:T(8,128)S(1)}, u32[]{:S(2)}, u32[]{:S(2)}) async-start(f32[8,32,1,128]{3,1,2,0:T(8,128)} %constant_dynamic-update-slice_fusion), calls=%async_computation.2 | async-start | bytes 262144 | tf_op jit(solution)/shard_map/all_to_all | solution.py:76
  110.1 7.3 %all-to-all-done.1 = f32[8,32,1,128]{3,1,2,0:T(8,128)S(1)} async-done(((f32[8,32,1,128]{3,1,2,0:T(8,128)}), f32[8,32,1,128]{3,1,2,0:T(8,128)S(1)}, u32[]{:S(2)}, u32[]{:S(2)}) %all-to-all-start.1) | async-done | bytes 131104 | tf_op jit(solution)/shard_map/all_to_all | solution.py:76
  118.1 3.1 %scatter_custom_fusion.2 = f32[32,4096]{0,1:T(8,128)S(1)} fusion(s32[512]{0:T(512)} %bitcast.230, f32[]{:T(128)} %constant.82.clone.1, f32[32,512]{0,1:T(8,128)S(1)} %fusion.40), kind=kCustom, calls=%fused_computation.22 | custom fusion | flops 16384 | bytes 590336 | tf_op jit(solution)/shard_map/scatter-add | solution.py:40
  121.2 1.4 copy.98
  122.6 2.0 fusion.31
  124.6 13.7 %all-gather.5.cloned.1.call-done = bf16[128,4096]{1,0:T(8,128)(2,1)} async-done(((bf16[32,4096]{1,0:T(8,128)(2,1)}), bf16[128,4096]{1,0:T(8,128)(2,1)}) %all-gather.5.cloned.1.call-update) | async-done | bytes 1048592 | tf_op jit(solution)/shard_map/all_gather | solution.py:43
  138.3 11.4 %fusion = f32[128,4096]{1,0:T(8,128)} fusion(bf16[1,1024,4096]{2,1,0:T(8,128)(2,1)} %param.7, bf16[128,4096]{1,0:T(8,128)(2,1)} %all-gather.5.cloned.1.call-done, f32[1024]{0:T(1024)S(1)} %fusion.57), kind=kOutput, calls=%fused_computation.10 | convolution fusion | flops 2147745792 | bytes 11538432 | tf_op jit(solution)/shard_map/dot_general | solution.py:50
  149.9 31.1 %reduce-scatter.5.cloned.1.call-done = f32[32,4096]{1,0:T(8,128)} async-done(((f32[128,4096]{1,0:T(8,128)}), f32[32,4096]{1,0:T(8,128)}) %reduce-scatter.5.cloned.1.call-update) | async-done | bytes 524304 | tf_op jit(solution)/shard_map/reduce_scatter | solution.py:49
  181.0 1.1 broadcast_multiply_fusion
  182.7 1.0 gather_fusion.3
  184.6 14.1 %all_to_all.20 = f32[2,32,8,128]{3,1,0,2:T(8,128)S(1)} all-to-all(f32[2,32,8,128]{3,1,0,2:T(8,128)S(1)} %copy.104), channel_id=1, replica_groups=mesh['area'=8,'scen'=4] {'area'}, dimensions={2} | all-to-all | bytes 524288 | tf_op jit(solution)/shard_map/all_to_all | solution.py:69
  199.3 4.0 %gather_fusion.4 = f32[1024,2,32]{2,1,0:T(2,128)S(1)} fusion(f32[2,32,1024]{1,0,2:T(2,128)S(1)} %bitcast.203, s32[1024]{0:T(1024)} %copy-done.3), kind=kCustom, calls=%fused_computation.4 | custom fusion | bytes 528384 | tf_op jit(solution)/shard_map/gather | solution.py:71
  209.7 3.6 %all-to-all-start.3 = ((f32[8,32,1,128]{3,1,2,0:T(8,128)}), f32[8,32,1,128]{3,1,2,0:T(8,128)S(1)}, u32[]{:S(2)}, u32[]{:S(2)}) async-start(f32[8,32,1,128]{3,1,2,0:T(8,128)} %constant_dynamic-update-slice_fusion.8), calls=%async_computation.5 | async-start | bytes 262144 | tf_op jit(solution)/shard_map/all_to_all | solution.py:76
  214.1 6.5 %all-to-all-done.3 = f32[8,32,1,128]{3,1,2,0:T(8,128)S(1)} async-done(((f32[8,32,1,128]{3,1,2,0:T(8,128)}), f32[8,32,1,128]{3,1,2,0:T(8,128)S(1)}, u32[]{:S(2)}, u32[]{:S(2)}) %all-to-all-start.3) | async-done | bytes 131104 | tf_op jit(solution)/shard_map/all_to_all | solution.py:76
  (95 shorter events, 27.5 us)
Async XLA Ops:
  7.2 27.4 %all-gather.3.cloned.1.call-start = ((), (), s32[]{:S(2)}) async-start(), calls=%async_computation.6 | async-start | bytes 1310720 | tf_op jit(solution)/shard_map/all_gather | solution.py:43
  9.2 37.6 %copy-start.8 = (s32[512,1]{0,1:T(1,128)}, s32[512,1]{0,1:T(1,128)S(1)}, u32[]{:S(2)}) copy-start(s32[512,1]{0,1:T(1,128)S(1)} %compare_select_fusion.1) | copy-start | bytes 6148
  10.8 3.4 %copy-start.1 = (f32[1,32,4096]{2,1,0:T(8,128)S(1)}, f32[1,32,4096]{2,1,0:T(8,128)}, u32[]{:S(2)}) copy-start(f32[1,32,4096]{2,1,0:T(8,128)} %param.6) | copy-start | bytes 1572868
  15.0 62.4 %reduce-scatter.3.cloned.1.call-start = ((), (), s32[]{:S(2)}) async-start(), calls=%async_computation.7 | async-start | bytes 2621440 | tf_op jit(solution)/shard_map/reduce_scatter | solution.py:49
  46.0 0.9 copy-start.2
  46.8 33.3 %copy-start.4 = (s32[1024]{0:T(1024)}, s32[1024]{0:T(1024)S(1)}, u32[]{:S(2)}) copy-start(s32[1024]{0:T(1024)S(1)} %pad_clamp_fusion.1) | copy-start | bytes 12292
  46.9 63.1 %copy-start.6 = (s32[4]{0:T(128)}, s32[4]{0:T(128)S(1)}, u32[]{:S(2)}) copy-start(s32[4]{0:T(128)S(1)} %fusion.65) | copy-start | bytes 52
  81.6 14.3 %all-to-all-start = ((f32[2,32,8,128]{3,1,0,2:T(8,128)}), f32[2,32,8,128]{3,1,0,2:T(8,128)S(1)}, u32[]{:S(2)}, u32[]{:S(2)}) async-start(f32[2,32,8,128]{3,1,0,2:T(8,128)} %copy.83), calls=%async_computation.1 | async-start | bytes 524288 | tf_op jit(solution)/shard_map/all_to_all | solution.py:69
  87.9 13.2 %copy-start.3 = (s32[1024]{0:T(1024)}, s32[1024]{0:T(1024)S(1)}, u32[]{:S(2)}) copy-start(s32[1024]{0:T(1024)S(1)} %broadcast_clamp_fusion) | copy-start | bytes 12292
  106.4 10.9 %all-to-all-start.1 = ((f32[8,32,1,128]{3,1,2,0:T(8,128)}), f32[8,32,1,128]{3,1,2,0:T(8,128)S(1)}, u32[]{:S(2)}, u32[]{:S(2)}) async-start(f32[8,32,1,128]{3,1,2,0:T(8,128)} %constant_dynamic-update-slice_fusion), calls=%async_computation.2 | async-start | bytes 262144 | tf_op jit(solution)/shard_map/all_to_all | solution.py:76
  110.0 28.2 %all-gather.5.cloned.1.call-start = ((), (), s32[]{:S(2)}) async-start(), calls=%async_computation.8 | async-start | bytes 1310720 | tf_op jit(solution)/shard_map/all_gather | solution.py:43
  110.1 12.5 %copy-start.9 = (s32[1024]{0:T(1024)}, s32[1024]{0:T(1024)S(1)}, u32[]{:S(2)}) copy-start(s32[1024]{0:T(1024)S(1)} %pad_clamp_fusion) | copy-start | bytes 12292
  124.5 56.5 %reduce-scatter.5.cloned.1.call-start = ((), (), s32[]{:S(2)}) async-start(), calls=%async_computation.9 | async-start | bytes 2621440 | tf_op jit(solution)/shard_map/reduce_scatter | solution.py:49
  149.7 33.0 %copy-start.5 = (s32[1024]{0:T(1024)S(1)}, s32[1024]{0:T(1024)}, u32[]{:S(2)}) copy-start(s32[1024]{0:T(1024)} %copy-done.4) | copy-start | bytes 12292
  182.1 1.8 copy-start.7
  204.1 9.1 %copy-start = (f32[32,4096]{1,0:T(8,128)S(1)}, f32[32,4096]{1,0:T(8,128)}, u32[]{:S(2)}) copy-start(f32[32,4096]{1,0:T(8,128)} %reduce-scatter.5.cloned.1.call-done) | copy-start | bytes 1572868
  209.7 10.9 %all-to-all-start.3 = ((f32[8,32,1,128]{3,1,2,0:T(8,128)}), f32[8,32,1,128]{3,1,2,0:T(8,128)S(1)}, u32[]{:S(2)}, u32[]{:S(2)}) async-start(f32[8,32,1,128]{3,1,2,0:T(8,128)} %constant_dynamic-update-slice_fusion.8), calls=%async_computation.5 | async-start | bytes 262144 | tf_op jit(solution)/shard_map/all_to_all | solution.py:76
Sparse Core Ops, SparseCore 0:
  15.1 19.4 all-gather.2
  46.1 31.1 reduce-scatter.2
  124.7 13.5 all-gather.4
  149.8 31.1 reduce-scatter.4
